TPU v7x, 32 devices: a whole 2x2x4 slice. The times are simulated.
32 devices in a mesh: grp: 4 (over y, x), dp: 8 (over z, core).
Axes of the slice: x: 2, y: 2, z: 4, core: 2. Of those that a mesh axis runs over, the one named last changes fastest.
Arguments:
- pixels: bfloat16 [4, 64, 256, 1024], P('grp', 'dp'), may hold values from -6 to 6
- keep_index: int32 [4, 64, 64], P('grp', 'dp'), may hold values from 0 to 255, as said below
- band_group: int32 [4, 64, 256], P('grp', 'dp'), may hold values from 0 to 3, as said below
- gsd_index: int32 [4, 64, 256], P('grp', 'dp'), may hold values from 0 to 511
- gsd_table: float32 [4, 512, 1536], P('grp'), may hold values from -4 to 4
- group_items: int32 [4], P('grp'), may hold values from 32 to 64, as said below
- step_count: int32 [1], replicated, may hold values from 2 to 20
- enc_cols: float32 [1024, 8192], P('dp'), may hold values from -0.1875 to 0.1875
- enc_rows: float32 [8192, 1024], P('dp'), may hold values from -0.09375 to 0.09375
- dec_cols: float32 [512, 4096], P('dp'), may hold values from -0.25 to 0.25
- dec_rows: float32 [4096, 512], P('dp'), may hold values from -0.1875 to 0.1875
- enc_gains: float32 [6, 1024], replicated
- dec_gains: float32 [7, 512], replicated
- moment_ecols: float32 [1024, 8192], P('dp'), may hold values from -1.5258789e-05 to 1.5258789e-05
- moment_erows: float32 [8192, 1024], P('dp'), may hold values from -1.5258789e-05 to 1.5258789e-05
- moment_dcols: float32 [512, 4096], P('dp'), may hold values from -1.5258789e-05 to 1.5258789e-05
- moment_drows: float32 [4096, 512], P('dp'), may hold values from -1.5258789e-05 to 1.5258789e-05
- moment_egains: float32 [6, 1024], replicated, may hold values from -3.0517578e-05 to 3.0517578e-05
- moment_dgains: float32 [7, 512], replicated, may hold values from -3.0517578e-05 to 3.0517578e-05
- square_ecols: float32 [1024, 8192], P('dp'), may hold values from 1.1915401e-12 to 4.7661606e-12
- square_erows: float32 [8192, 1024], P('dp'), may hold values from 1.1915401e-12 to 4.7661606e-12
- square_dcols: float32 [512, 4096], P('dp'), may hold values from 1.1915401e-12 to 4.7661606e-12
- square_drows: float32 [4096, 512], P('dp'), may hold values from 1.1915401e-12 to 4.7661606e-12
- square_egains: float32 [6, 1024], replicated, may hold values from 2.3830803e-12 to 9.532321e-12
- square_dgains: float32 [7, 512], replicated, may hold values from 2.3830803e-12 to 9.532321e-12
Outputs:
- clipped_ecols: float32 [1024, 8192], P('dp')
- squares_ecols: float32 [1024, 8192], P('dp')
- updated_ecols: float32 [1024, 8192], P('dp')
- clipped_erows: float32 [8192, 1024], P('dp')
- squares_erows: float32 [8192, 1024], P('dp')
- updated_erows: float32 [8192, 1024], P('dp')
- clipped_dcols: float32 [512, 4096], P('dp')
- squares_dcols: float32 [512, 4096], P('dp')
- updated_dcols: float32 [512, 4096], P('dp')
- clipped_drows: float32 [4096, 512], P('dp')
- squares_drows: float32 [4096, 512], P('dp')
- updated_drows: float32 [4096, 512], P('dp')
- clipped_egains: float32 [6, 1024], replicated
- squares_egains: float32 [6, 1024], replicated
- updated_egains: float32 [6, 1024], replicated
- clipped_dgains: float32 [7, 512], replicated
- squares_dgains: float32 [7, 512], replicated
- updated_dgains: float32 [7, 512], replicated
- loss: float32 [], replicated
- grad_norm: float32 [], replicated
Inputs may be any that keep to these rules, and one draw needn't show every extreme that they name: `keep_index`: each item's 64 entries are distinct patch positions. `band_group`: in groups of odd index every entry is 3. `group_items`: one group uses all 64 slots and another group 64 // 2.
All inputs are finite; a program needn't handle non-finite values.
Results may differ from a plain program's by a relative error of at most 0.017.
Values may be sent and summed in bfloat16 or wider, within the bound.
A program may use at most 384 MiB of HBM per device.

v0:
```python
import jax
import jax.numpy as jnp
from jax import lax
from jax.sharding import PartitionSpec as P

D = 1024
HEADS = 16
FF = 4096
DHEADS = 16
DFF = 2048
PIX = 1024
NBG = 4
L = 256
K = 64
norm_eps = 1e-06
clip_level = 0.005
learn_rate = 0.02
gain_rate = 0.25
weight_decay = 0.05
adam_eps = 1e-08
beta_first = 0.5
beta_second = 0.5


def to_low(value):
    return value.astype(jnp.bfloat16)


def project(inputs, matrix):
    return jnp.einsum("...n,nm->...m", inputs, matrix, preferred_element_type=jnp.float32)


def project_back(grads, matrix):
    return jnp.einsum("...m,nm->...n", grads, matrix, preferred_element_type=jnp.float32)


def weight_grad(inputs, grads):
    flat_in = inputs.reshape(-1, inputs.shape[-1])
    flat_grad = grads.reshape(-1, grads.shape[-1])
    return lax.dot_general(
        flat_in, flat_grad, (((0,), (0,)), ((), ())), preferred_element_type=jnp.float32
    )


def norm_forward(values, gain, shift):
    centred = values - jnp.mean(values, -1, keepdims=True)
    scaled = lax.rsqrt(jnp.mean(centred * centred, -1, keepdims=True) + norm_eps)
    normed = centred * scaled
    return (normed * gain + shift, normed, scaled)


def norm_backward(grads, normed, scaled, gain):
    inner = grads * gain
    back = scaled * (
        inner
        - jnp.mean(inner, -1, keepdims=True)
        - normed * jnp.mean(inner * normed, -1, keepdims=True)
    )
    flat_grad = grads.reshape(-1, grads.shape[-1])
    flat_norm = normed.reshape(-1, normed.shape[-1])
    return (back, jnp.sum(flat_grad * flat_norm, 0), jnp.sum(flat_grad, 0))


def gelu_parts(hidden):
    cumul = 0.5 * (1.0 + jax.scipy.special.erf(hidden * 0.7071067811865476))
    return (hidden * cumul, cumul + hidden * jnp.exp(-0.5 * hidden * hidden) * 0.3989422804014327)


def split_heads(packed, width, heads):
    shape = (packed.shape[0], packed.shape[1], heads, width // heads)
    return (
        packed[..., :width].reshape(shape),
        packed[..., width : 2 * width].reshape(shape),
        packed[..., 2 * width :].reshape(shape),
    )


def head_scores(queries, key_part, scale):
    return (
        jnp.einsum("bqhe,bkhe->bhqk", queries, key_part, preferred_element_type=jnp.float32) * scale
    )


def block_forward(inputs, columns, down_rows, gains, heads):
    width = inputs.shape[-1]
    scale = (width // heads) ** (-0.5)
    normed_one, hat_one, scale_one = norm_forward(inputs, gains[0], gains[1])
    first_in = to_low(normed_one)
    packed = to_low(project(first_in, columns[:, : 3 * width]))
    queries, key_part, val_part = split_heads(packed, width, heads)
    scores = head_scores(queries, key_part, scale)
    log_total = jax.nn.logsumexp(scores, -1, keepdims=True)
    attn_prob = to_low(jnp.exp(scores - log_total))
    mixed = jnp.einsum("bhqk,bkhe->bqhe", attn_prob, val_part, preferred_element_type=jnp.float32)
    mixed = to_low(mixed.reshape(inputs.shape))
    middle = inputs + project(mixed, columns[:, 3 * width : 4 * width])
    normed_two, hat_two, scale_two = norm_forward(middle, gains[2], gains[3])
    second_in = to_low(normed_two)
    hidden = project(second_in, columns[:, 4 * width :])
    activated = to_low(gelu_parts(hidden)[0])
    output = middle + project(activated, down_rows)
    saved = (
        hat_one,
        scale_one,
        first_in,
        packed,
        log_total,
        mixed,
        hat_two,
        scale_two,
        second_in,
        hidden,
        activated,
    )
    return (output, saved)


def block_backward(grad_out, columns, down_rows, gains, heads, saved):
    (
        hat_one,
        scale_one,
        first_in,
        packed,
        log_total,
        mixed,
        hat_two,
        scale_two,
        second_in,
        hidden,
        activated,
    ) = saved
    width = grad_out.shape[-1]
    scale = (width // heads) ** (-0.5)
    grad_low = to_low(grad_out)
    grad_down = weight_grad(activated, grad_low)
    grad_hidden = to_low(project_back(grad_low, down_rows) * gelu_parts(hidden)[1])
    grad_up = weight_grad(second_in, grad_hidden)
    back_two, gain_two, shift_two = norm_backward(
        project_back(grad_hidden, columns[:, 4 * width :]), hat_two, scale_two, gains[2]
    )
    grad_middle = grad_out + back_two
    middle_low = to_low(grad_middle)
    grad_proj = weight_grad(mixed, middle_low)
    head_shape = packed.shape[:2] + (heads, width // heads)
    grad_mixed = to_low(
        project_back(middle_low, columns[:, 3 * width : 4 * width]).reshape(head_shape)
    )
    queries, key_part, val_part = split_heads(packed, width, heads)
    attn_prob = jnp.exp(head_scores(queries, key_part, scale) - log_total)
    grad_prob = jnp.einsum(
        "bqhe,bkhe->bhqk", grad_mixed, val_part, preferred_element_type=jnp.float32
    )
    grad_val = jnp.einsum(
        "bhqk,bqhe->bkhe", to_low(attn_prob), grad_mixed, preferred_element_type=jnp.float32
    )
    grad_score = to_low(attn_prob * (grad_prob - jnp.sum(grad_prob * attn_prob, -1, keepdims=True)))
    grad_query = (
        jnp.einsum("bhqk,bkhe->bqhe", grad_score, key_part, preferred_element_type=jnp.float32)
        * scale
    )
    grad_key = (
        jnp.einsum("bhqk,bqhe->bkhe", grad_score, queries, preferred_element_type=jnp.float32)
        * scale
    )
    flat_shape = packed.shape[:2] + (width,)
    grad_packed = to_low(
        jnp.concatenate(
            [
                grad_query.reshape(flat_shape),
                grad_key.reshape(flat_shape),
                grad_val.reshape(flat_shape),
            ],
            -1,
        )
    )
    grad_qkv = weight_grad(first_in, grad_packed)
    back_one, gain_one, shift_one = norm_backward(
        project_back(grad_packed, columns[:, : 3 * width]), hat_one, scale_one, gains[0]
    )
    grad_in = grad_middle + back_one
    grad_cols = jnp.concatenate([grad_qkv, grad_proj, grad_up], 1)
    grad_gains = jnp.stack([gain_one, shift_one, gain_two, shift_two])
    return (grad_in, grad_cols, grad_down, grad_gains)


def adam_step(master, moment, square, grad, factor, fix_one, fix_two, decay, rate):
    clipped = grad * factor
    moment_new = beta_first * moment + (1.0 - beta_first) * clipped
    square_new = beta_second * square + (1.0 - beta_second) * clipped * clipped
    direction = moment_new / fix_one / (jnp.sqrt(square_new / fix_two) + adam_eps) + decay * master
    return (clipped, square_new, master - rate * direction)


def body(
    pixels,
    keep_index,
    band_group,
    gsd_index,
    gsd_table,
    group_items,
    step_count,
    enc_cols,
    enc_rows,
    dec_cols,
    dec_rows,
    enc_gains,
    dec_gains,
    moment_ecols,
    moment_erows,
    moment_dcols,
    moment_drows,
    moment_egains,
    moment_dgains,
    square_ecols,
    square_erows,
    square_dcols,
    square_drows,
    square_egains,
    square_dgains,
):
    total_count = lax.psum(jnp.sum(group_items.astype(jnp.float32)), "grp")
    masked = total_count * (L - K)
    copies = (
        lax.all_gather(to_low(enc_cols), "dp", axis=0, tiled=True),
        lax.all_gather(to_low(enc_rows), "dp", axis=0, tiled=True),
        lax.all_gather(to_low(dec_cols), "dp", axis=0, tiled=True),
        lax.all_gather(to_low(dec_rows), "dp", axis=0, tiled=True),
    )
    enc_copy = copies[0]
    enc_down = copies[1][:FF]
    embed_w = copies[1][FF:]
    dec_copy = copies[2]
    dec_down = copies[3][:DFF]
    dec_embed = copies[3][DFF : DFF + D]
    head_rows = copies[3][DFF + D :]
    pixel_rows = pixels[0]
    keep_rows = keep_index[0]
    batch = pixel_rows.shape[0]
    kept_pixels = jnp.take_along_axis(pixel_rows, keep_rows[..., None], 1)
    kept_bands = jnp.take_along_axis(band_group[0], keep_rows, 1)
    onehot = (kept_bands[..., None] == jnp.arange(NBG, dtype=jnp.int32)).astype(jnp.bfloat16)
    spread = (onehot[..., None] * kept_pixels[:, :, None, :]).reshape(batch, K, NBG * PIX)
    position = jnp.take(gsd_table[0], gsd_index[0], axis=0)
    enc_input = project(spread, embed_w) + jnp.take_along_axis(
        position[..., :D], keep_rows[..., None], 1
    )
    enc_out, enc_saved = block_forward(enc_input, enc_copy, enc_down, enc_gains, HEADS)
    enc_final, enc_hat, enc_scale = norm_forward(enc_out, enc_gains[4], enc_gains[5])
    enc_low = to_low(enc_final)
    latent = project(enc_low, dec_embed)
    item_rows = jnp.arange(batch)[:, None]
    hidden_mask = jnp.ones((batch, L), jnp.float32).at[item_rows, keep_rows].set(0.0)
    dec_input = hidden_mask[..., None] * dec_gains[6] + position[..., D:]
    dec_input = dec_input.at[item_rows, keep_rows].add(latent)
    dec_out, dec_saved = block_forward(dec_input, dec_copy, dec_down, dec_gains, DHEADS)
    dec_final, dec_hat, dec_scale = norm_forward(dec_out, dec_gains[4], dec_gains[5])
    dec_low = to_low(dec_final)
    predicted = project_back(dec_low, head_rows)
    pixel_float = pixel_rows.astype(jnp.float32)
    centred = pixel_float - jnp.mean(pixel_float, -1, keepdims=True)
    target = centred * lax.rsqrt(jnp.mean(centred * centred, -1, keepdims=True) + norm_eps)
    first_item = lax.axis_index("dp") * batch
    valid = (first_item + jnp.arange(batch, dtype=jnp.int32) < group_items[0]).astype(jnp.float32)
    token_weight = hidden_mask * valid[:, None]
    error = predicted - target
    loss_local = jnp.sum(token_weight * jnp.mean(error * error, -1))
    grad_pred = to_low(token_weight[..., None] * error * (2.0 / PIX) / masked)
    grad_head = weight_grad(grad_pred, dec_low)
    back_dec, gain_df, shift_df = norm_backward(
        project(grad_pred, head_rows), dec_hat, dec_scale, dec_gains[4]
    )
    grad_dec_in, grad_dcols, grad_ddown, dec_block_gains = block_backward(
        back_dec, dec_copy, dec_down, dec_gains, DHEADS, dec_saved
    )
    grad_token = jnp.sum(grad_dec_in * hidden_mask[..., None], (0, 1))
    grad_latent = to_low(jnp.take_along_axis(grad_dec_in, keep_rows[..., None], 1))
    grad_dembed = weight_grad(enc_low, grad_latent)
    back_enc, gain_ef, shift_ef = norm_backward(
        project_back(grad_latent, dec_embed), enc_hat, enc_scale, enc_gains[4]
    )
    grad_enc_in, grad_ecols, grad_edown, enc_block_gains = block_backward(
        back_enc, enc_copy, enc_down, enc_gains, HEADS, enc_saved
    )
    grad_embed = weight_grad(spread, to_low(grad_enc_in))
    grads = (
        grad_ecols,
        jnp.concatenate([grad_edown, grad_embed], 0),
        grad_dcols,
        jnp.concatenate([grad_ddown, grad_dembed, grad_head], 0),
    )
    grad_egains = jnp.concatenate([enc_block_gains, jnp.stack([gain_ef, shift_ef])], 0)
    grad_dgains = jnp.concatenate([dec_block_gains, jnp.stack([gain_df, shift_df, grad_token])], 0)
    shards = (
        lax.psum_scatter(grads[0], "dp", scatter_dimension=0, tiled=True),
        lax.psum_scatter(grads[1], "dp", scatter_dimension=0, tiled=True),
        lax.psum_scatter(grads[2], "dp", scatter_dimension=0, tiled=True),
        lax.psum_scatter(grads[3], "dp", scatter_dimension=0, tiled=True),
    )
    shards = (
        lax.psum(shards[0].astype(jnp.bfloat16), "grp").astype(jnp.float32),
        lax.psum(shards[1].astype(jnp.bfloat16), "grp").astype(jnp.float32),
        lax.psum(shards[2].astype(jnp.bfloat16), "grp").astype(jnp.float32),
        lax.psum(shards[3].astype(jnp.bfloat16), "grp").astype(jnp.float32),
    )
    enc_sum, dec_sum, loss_sum = lax.psum((grad_egains, grad_dgains, loss_local), ("grp", "dp"))
    shard_squares = lax.psum(sum((jnp.sum(piece * piece) for piece in shards)), "dp")
    loss = loss_sum / masked
    grad_norm = jnp.sqrt(shard_squares + jnp.sum(enc_sum * enc_sum) + jnp.sum(dec_sum * dec_sum))
    factor = clip_level / jnp.maximum(grad_norm, clip_level)
    count_steps = step_count[0].astype(jnp.float32)
    fix_one = 1.0 - beta_first**count_steps
    fix_two = 1.0 - beta_second**count_steps
    clipped_ecols, squares_ecols, updated_ecols = adam_step(
        enc_cols,
        moment_ecols,
        square_ecols,
        shards[0],
        factor,
        fix_one,
        fix_two,
        weight_decay,
        learn_rate,
    )
    clipped_erows, squares_erows, updated_erows = adam_step(
        enc_rows,
        moment_erows,
        square_erows,
        shards[1],
        factor,
        fix_one,
        fix_two,
        weight_decay,
        learn_rate,
    )
    clipped_dcols, squares_dcols, updated_dcols = adam_step(
        dec_cols,
        moment_dcols,
        square_dcols,
        shards[2],
        factor,
        fix_one,
        fix_two,
        weight_decay,
        learn_rate,
    )
    clipped_drows, squares_drows, updated_drows = adam_step(
        dec_rows,
        moment_drows,
        square_drows,
        shards[3],
        factor,
        fix_one,
        fix_two,
        weight_decay,
        learn_rate,
    )
    clipped_egains, squares_egains, updated_egains = adam_step(
        enc_gains, moment_egains, square_egains, enc_sum, factor, fix_one, fix_two, 0.0, gain_rate
    )
    clipped_dgains, squares_dgains, updated_dgains = adam_step(
        dec_gains, moment_dgains, square_dgains, dec_sum, factor, fix_one, fix_two, 0.0, gain_rate
    )
    return (
        clipped_ecols,
        squares_ecols,
        updated_ecols,
        clipped_erows,
        squares_erows,
        updated_erows,
        clipped_dcols,
        squares_dcols,
        updated_dcols,
        clipped_drows,
        squares_drows,
        updated_drows,
        clipped_egains,
        squares_egains,
        updated_egains,
        clipped_dgains,
        squares_dgains,
        updated_dgains,
        loss,
        grad_norm,
    )


def solution(mesh):
    return jax.shard_map(
        body,
        mesh=mesh,
        in_specs=(
            P("grp", "dp", None, None),
            P("grp", "dp", None),
            P("grp", "dp", None),
            P("grp", "dp", None),
            P("grp", None, None),
            P("grp"),
            P(),
            P("dp", None),
            P("dp", None),
            P("dp", None),
            P("dp", None),
            P(),
            P(),
            P("dp", None),
            P("dp", None),
            P("dp", None),
            P("dp", None),
            P(),
            P(),
            P("dp", None),
            P("dp", None),
            P("dp", None),
            P("dp", None),
            P(),
            P(),
        ),
        out_specs=(
            P("dp", None),
            P("dp", None),
            P("dp", None),
            P("dp", None),
            P("dp", None),
            P("dp", None),
            P("dp", None),
            P("dp", None),
            P("dp", None),
            P("dp", None),
            P("dp", None),
            P("dp", None),
            P(),
            P(),
            P(),
            P(),
            P(),
            P(),
            P(),
            P(),
        ),
        check_vma=False,
    )
```

profile of v0, /device:TPU:0, one launch (start us, length us, event | category | flops | bytes accessed | tf_op | source)
XLA Modules:
  0.0 1718.9 jit_solution(14711521115183976709)
XLA Ops:
  20.2 12.5 psum.63
  43.0 10.9 gather_fusion.2
  66.9 11.0 gather_fusion
  77.9 10.1 broadcast_select_fusion
  96.4 10.5 gather_fusion.3
  108.0 24.3 %scatter_fusion = f32[8,256]{1,0:T(8,128)S(1)} fusion(f32[8,256]{1,0:T(8,128)S(1)} %broadcast_in_dim.52, s32[512]{0:T(512)S(1)} %reshape.496, f32[512]{0:T(512)S(1)} %broadcast.507), kind=kCustom, calls=%fused_computation.5 | custom fusion | bytes 10240 | tf_op jit(solution)/shard_map/scatter | solution.py:252
  137.0 28.3 %all-gather.5.cloned.1.call-done = bf16[8192,1024]{1,0:T(8,128)(2,1)} async-done(((bf16[1024,1024]{1,0:T(8,128)(2,1)}), bf16[8192,1024]{1,0:T(8,128)(2,1)}) %all-gather.5.cloned.1.call-update) | async-done | bytes 16777232 | tf_op jit(solution)/shard_map/all_gather | solution.py:225
  165.2 9.7 fusion.120
  175.4 141.4 %all-gather.7.cloned.1.call-done = bf16[1024,8192]{1,0:T(8,128)(2,1)} async-done(((bf16[128,8192]{1,0:T(8,128)(2,1)}), bf16[1024,8192]{1,0:T(8,128)(2,1)}) %all-gather.7.cloned.1.call-update) | async-done | bytes 16777232 | tf_op jit(solution)/shard_map/all_gather | solution.py:224
  346.2 10.8 multiply_convert_fusion.2
  366.3 64.7 %scatter_fusion.1 = f32[8,256,512]{2,1,0:T(8,128)} fusion(f32[8,256,512]{2,1,0:T(8,128)} %slice_add_fusion, s32[512]{0:T(512)S(1)} %reshape.496, f32[512,512]{1,0:T(8,128)S(1)} %bitcast.272), kind=kCustom, calls=%fused_computation.6 | custom fusion | flops 262144 | bytes 3149824 | tf_op jit(solution)/shard_map/scatter-add | solution.py:254
  455.9 14.4 multiply_reduce_fusion.1
  470.3 13.8 exponential_reduce_fusion
  484.2 15.7 fusion.42
  506.5 9.3 multiply_convert_fusion.1
  544.2 13.8 fusion.6
  582.5 15.9 fusion.45
  598.4 23.3 %multiply_reduce_fusion = (f32[8,16,256]{2,1,0:T(8,128)S(1)}, f32[8,16,256,256]{2,3,1,0:T(8,128)}) fusion(f32[8,16,256,256]{2,3,1,0:T(8,128)} %get-tuple-element.107, f32[8,16,256]{2,1,0:T(8,128)S(1)} %log_add_fusion, bf16[8,256,16,32]{1,3,2,0:T(8,128)(2,1)} %bitcast.251, bf16[8,256,16,32]{1,3,2,0:T(8,128)(2,1)S(1)} %bitcast.249), kind=kOutput, calls=%fused_computation.10 | convolution fusion | flops 570392576 | bytes 71565312 | tf_op jit(solution)/shard_map/bqhe,bkhe->bhqk/dot_general | solution.py:150
  621.7 28.0 %multiply_convert_fusion = bf16[8,16,256,256]{2,3,1,0:T(8,128)(2,1)} fusion(f32[8,16,256,256]{2,3,1,0:T(8,128)} %get-tuple-element.119, f32[8,16,256,256]{2,3,1,0:T(8,128)} %get-tuple-element.107, f32[8,16,256]{2,1,0:T(8,128)S(1)} %get-tuple-element.118, f32[8,16,256]{2,1,0:T(8,128)S(1)} %log_add_fusion), kind=kLoop, calls=%fused_computation.9 | loop fusion | flops 41943040 | bytes 84148224 | tf_op jit(solution)/shard_map/convert_element_type | solution.py:26
  649.7 12.0 multiply_convert_fusion.6
  661.7 10.5 multiply_convert_fusion.7
  732.6 11.0 fusion.16
  743.7 9.7 multiply_reduce_fusion.19
  810.5 22.9 %pad_maximum_fusion = f32[1024,8192]{1,0:T(8,128)} fusion(f32[1024,4096]{1,0:T(8,128)} %convolution_bitcast_fusion.1, f32[1024,1024]{1,0:T(8,128)} %convolution_bitcast_fusion.6, f32[1024,3072]{1,0:T(8,128)} %convolution_bitcast_fusion.2), kind=kLoop, calls=%fused_computation.7 | loop fusion | flops 16777216 | bytes 67108864 | tf_op jit(solution)/shard_map/concatenate | solution.py:181
  850.7 8.8 convolution_bitcast_fusion
  859.5 18.8 %pad_maximum_fusion.1 = f32[8192,1024]{1,0:T(8,128)} fusion(f32[4096,1024]{1,0:T(8,128)S(1)} %fusion.125, f32[4096,1024]{1,0:T(8,128)} %convolution_bitcast_fusion), kind=kLoop, calls=%fused_computation.8 | loop fusion | flops 8388608 | bytes 67108864 | tf_op jit(solution)/shard_map/concatenate | solution.py:287
  882.7 316.6 %reduce-scatter.5.cloned.1.call-done = f32[128,8192]{1,0:T(8,128)} async-done(((f32[1024,8192]{1,0:T(8,128)}), f32[128,8192]{1,0:T(8,128)}) %reduce-scatter.5.cloned.1.call-update) | async-done | bytes 4194320 | tf_op jit(solution)/shard_map/reduce_scatter | solution.py:294
  1203.0 322.7 %reduce-scatter.7.cloned.1.call-done = f32[1024,1024]{1,0:T(8,128)} async-done(((f32[8192,1024]{1,0:T(8,128)}), f32[1024,1024]{1,0:T(8,128)}) %reduce-scatter.7.cloned.1.call-update) | async-done | bytes 4194320 | tf_op jit(solution)/shard_map/reduce_scatter | solution.py:295
  1530.7 38.8 %all-reduce = (f32[6,1024]{1,0:T(8,128)S(1)}, f32[7,512]{1,0:T(8,128)S(1)}, f32[]{:T(128)}) all-reduce(f32[6,1024]{1,0:T(8,128)S(1)} %concatenate.37, f32[7,512]{1,0:T(8,128)S(1)} %concatenate.38, f32[]{:T(128)} %get-tuple-element.69), channel_id=1, replica_groups=mesh['grp'=4,'dp'=8] {'grp','dp'}, use_global_device_ids=true, to_apply=%region_54.55 | all-reduce | flops 9729 | bytes 77832 | tf_op jit(solution)/shard_map/psum | solution.py:305
  1570.7 81.2 %all-reduce.4.cloned.1.call-done = (bf16[128,8192]{1,0:T(8,128)(2,1)}, bf16[1024,1024]{1,0:T(8,128)(2,1)}, bf16[64,4096]{1,0:T(8,128)(2,1)}, bf16[512,512]{1,0:T(8,128)(2,1)}) async-done(((bf16[128,8192]{1,0:T(8,128)(2,1)}, bf16[1024,1024]{1,0:T(8,128)(2,1)}, bf16[64,4096]{1,0:T(8,128)(2,1)}, bf16[512,512]{1,0:T(8,128)(2,1)}), (bf16[128,8192]{1,0:T(8,128)(2,1)}, bf16[1024,1024]{1,0:T(8,128)(2,1)}, ...) | async-done | bytes 5242896 | tf_op jit(solution)/shard_map/psum | solution.py:300
  1664.1 17.0 psum.68
  1693.5 8.9 fusion.35
  (451 shorter events, 345.9 us)
Async XLA Ops:
  7.2 59.7 %copy-start = (f32[1,512,1536]{2,1,0:T(8,128)S(1)}, f32[1,512,1536]{2,1,0:T(8,128)}, u32[]{:S(2)}) copy-start(f32[1,512,1536]{2,1,0:T(8,128)} %param.29) | copy-start | bytes 9437188
  7.2 158.0 %all-gather.5.cloned.1.call-start = ((), (), s32[]{:S(2)}) async-start(), calls=%async_computation.4 | async-start | bytes 18874368 | tf_op jit(solution)/shard_map/all_gather | solution.py:225
  11.3 305.5 %all-gather.7.cloned.1.call-start = ((), (), s32[]{:S(2)}) async-start(), calls=%async_computation.5 | async-start | bytes 18874368 | tf_op jit(solution)/shard_map/all_gather | solution.py:224
  15.1 349.2 %all-gather.9.cloned.1.call-start = ((), (), s32[]{:S(2)}) async-start(), calls=%async_computation.6 | async-start | bytes 4718592 | tf_op jit(solution)/shard_map/all_gather | solution.py:227
  17.3 419.3 %all-gather.11.cloned.1.call-start = ((), (), s32[]{:S(2)}) async-start(), calls=%async_computation.7 | async-start | bytes 4718592 | tf_op jit(solution)/shard_map/all_gather | solution.py:226
  19.4 859.0 %reduce-scatter.9.cloned.1.call-start = ((), (), s32[]{:S(2)}) async-start(), calls=%async_computation.10 | async-start | bytes 9437184 | tf_op jit(solution)/shard_map/reduce_scatter | solution.py:296
  42.1 123.1 %copy-start.108 = (pred[8,64]{1,0:T(8,128)(4,1)}, pred[8,64]{1,0:T(8,128)(4,1)S(1)}, u32[]{:S(2)}) copy-start(pred[8,64]{1,0:T(8,128)(4,1)S(1)} %get-tuple-element.74) | copy-start | bytes 1540
  42.7 393.8 %copy-start.105 = (f32[1,512]{1,0:T(1,128)}, f32[1,512]{1,0:T(1,128)S(1)}, u32[]{:S(2)}) copy-start(f32[1,512]{1,0:T(1,128)S(1)} %get-tuple-element.91) | copy-start | bytes 6148
  42.7 393.8 %copy-start.120 = (f32[1,512]{1,0:T(1,128)}, f32[1,512]{1,0:T(1,128)S(1)}, u32[]{:S(2)}) copy-start(f32[1,512]{1,0:T(1,128)S(1)} %get-tuple-element.90) | copy-start | bytes 6148
  42.8 274.0 %copy-start.61 = (f32[1,1024]{1,0:T(1,128)}, f32[1,1024]{1,0:T(1,128)S(1)}, u32[]{:S(2)}) copy-start(f32[1,1024]{1,0:T(1,128)S(1)} %get-tuple-element.85) | copy-start | bytes 12292
  42.8 274.0 %copy-start.65 = (f32[1,1024]{1,0:T(1,128)}, f32[1,1024]{1,0:T(1,128)S(1)}, u32[]{:S(2)}) copy-start(f32[1,1024]{1,0:T(1,128)S(1)} %get-tuple-element.84) | copy-start | bytes 12292
  42.8 303.4 %copy-start.92 = (f32[1,1024]{1,0:T(1,128)}, f32[1,1024]{1,0:T(1,128)S(1)}, u32[]{:S(2)}) copy-start(f32[1,1024]{1,0:T(1,128)S(1)} %get-tuple-element.83) | copy-start | bytes 12292
  42.8 303.4 %copy-start.114 = (f32[1,1024]{1,0:T(1,128)}, f32[1,1024]{1,0:T(1,128)S(1)}, u32[]{:S(2)}) copy-start(f32[1,1024]{1,0:T(1,128)S(1)} %get-tuple-element.82) | copy-start | bytes 12292
  42.8 321.5 %copy-start.99 = (f32[1,1024]{1,0:T(1,128)}, f32[1,1024]{1,0:T(1,128)S(1)}, u32[]{:S(2)}) copy-start(f32[1,1024]{1,0:T(1,128)S(1)} %get-tuple-element.81) | copy-start | bytes 12292
  42.8 321.5 %copy-start.116 = (f32[1,1024]{1,0:T(1,128)}, f32[1,1024]{1,0:T(1,128)S(1)}, u32[]{:S(2)}) copy-start(f32[1,1024]{1,0:T(1,128)S(1)} %get-tuple-element.86) | copy-start | bytes 12292
  175.0 167.1 %copy-start.17 = (f32[8,64,1024]{2,1,0:T(8,128)}, f32[8,64,1024]{2,1,0:T(8,128)S(1)}, u32[]{:S(2)}) copy-start(f32[8,64,1024]{2,1,0:T(8,128)S(1)} %get-tuple-element.97) | copy-start | bytes 6291460
  175.0 148.4 %copy-start.59 = (f32[8,64]{1,0:T(8,128)}, f32[8,64]{1,0:T(8,128)S(1)}, u32[]{:S(2)}) copy-start(f32[8,64]{1,0:T(8,128)S(1)} %broadcast_multiply_fusion.22) | copy-start | bytes 6148
  175.4 148.0 %copy-start.63 = (f32[8,64]{1,0:T(8,128)}, f32[8,64]{1,0:T(8,128)S(1)}, u32[]{:S(2)}) copy-start(f32[8,64]{1,0:T(8,128)S(1)} %add_rsqrt_fusion.6) | copy-start | bytes 6148
  362.6 68.4 %copy-start.37 = (f32[8,64,1024]{2,1,0:T(8,128)}, f32[8,64,1024]{2,1,0:T(8,128)S(1)}, u32[]{:S(2)}) copy-start(f32[8,64,1024]{2,1,0:T(8,128)S(1)} %get-tuple-element.105) | copy-start | bytes 6291460
  362.6 68.4 %copy-start.80 = (f32[8,64]{1,0:T(8,128)}, f32[8,64]{1,0:T(8,128)S(1)}, u32[]{:S(2)}) copy-start(f32[8,64]{1,0:T(8,128)S(1)} %broadcast_multiply_fusion.20) | copy-start | bytes 6148
  363.0 68.0 %copy-start.101 = (f32[8,64]{1,0:T(8,128)}, f32[8,64]{1,0:T(8,128)S(1)}, u32[]{:S(2)}) copy-start(f32[8,64]{1,0:T(8,128)S(1)} %add_rsqrt_fusion.4) | copy-start | bytes 6148
  694.3 186.2 %reduce-scatter.11.cloned.1.call-start = ((), (), s32[]{:S(2)}) async-start(), calls=%async_computation.11 | async-start | bytes 9437184 | tf_op jit(solution)/shard_map/reduce_scatter | solution.py:297
  727.3 471.9 %reduce-scatter.5.cloned.1.call-start = ((), (), s32[]{:S(2)}) async-start(), calls=%async_computation.8 | async-start | bytes 37748736 | tf_op jit(solution)/shard_map/reduce_scatter | solution.py:294
  833.4 692.2 %reduce-scatter.7.cloned.1.call-start = ((), (), s32[]{:S(2)}) async-start(), calls=%async_computation.9 | async-start | bytes 37748736 | tf_op jit(solution)/shard_map/reduce_scatter | solution.py:295
  878.3 773.6 %all-reduce.4.cloned.1.call-start = ((), (), s32[]{:S(2)}) async-start(), calls=%async_computation.12 | async-start | bytes 10485760 | tf_op jit(solution)/shard_map/psum | solution.py:300
  1529.6 153.6 %copy-start.77 = (f32[7,512]{1,0:T(8,128)S(1)}, f32[7,512]{1,0:T(8,128)}, u32[]{:S(2)}) copy-start(f32[7,512]{1,0:T(8,128)} %param.37) | copy-start | bytes 43012
  1529.6 153.6 %copy-start.96 = (f32[7,512]{1,0:T(8,128)S(1)}, f32[7,512]{1,0:T(8,128)}, u32[]{:S(2)}) copy-start(f32[7,512]{1,0:T(8,128)} %param.43) | copy-start | bytes 43012
  1529.6 153.6 %copy-start.97 = (f32[7,512]{1,0:T(8,128)S(1)}, f32[7,512]{1,0:T(8,128)}, u32[]{:S(2)}) copy-start(f32[7,512]{1,0:T(8,128)} %param.49) | copy-start | bytes 43012
  1529.6 154.2 %copy-start.69 = (f32[6,1024]{1,0:T(8,128)S(1)}, f32[6,1024]{1,0:T(8,128)}, u32[]{:S(2)}) copy-start(f32[6,1024]{1,0:T(8,128)} %param.36) | copy-start | bytes 73732
  1529.6 154.2 %copy-start.85 = (f32[6,1024]{1,0:T(8,128)S(1)}, f32[6,1024]{1,0:T(8,128)}, u32[]{:S(2)}) copy-start(f32[6,1024]{1,0:T(8,128)} %param.42) | copy-start | bytes 73732
  1529.6 154.2 %copy-start.86 = (f32[6,1024]{1,0:T(8,128)S(1)}, f32[6,1024]{1,0:T(8,128)}, u32[]{:S(2)}) copy-start(f32[6,1024]{1,0:T(8,128)} %param.48) | copy-start | bytes 73732
  1529.7 154.8 %copy-start.49 = (f32[512,512]{1,0:T(8,128)S(1)}, f32[512,512]{1,0:T(8,128)}, u32[]{:S(2)}) copy-start(f32[512,512]{1,0:T(8,128)} %param.35) | copy-start | bytes 3145732
  (119 other events, 809.7 us)
Sparse Core Ops, SparseCore 0:
  11.4 153.7 all-gather.4
  167.4 149.3 all-gather.6
  318.9 45.3 all-gather.8
  366.4 45.8 all-gather.10
  694.4 88.3 reduce-scatter.8
  784.9 87.9 reduce-scatter.10
  875.3 323.8 reduce-scatter.4
  1201.7 323.8 reduce-scatter.6
  1530.6 121.2 all-reduce.3
where the time goes:
time: 1730 us; the launch traced here: 1720 us
  waiting for transfers between devices  892 us (52%)
  matrix products  310 us (18%)
  other arithmetic  265 us (15%)
  local copies, waits for them, and re-layouts  157 us (9%)
  blocking collectives  68.3 us (4%)
  between operations  25.6 us (1%)
    reduce_scatter x1, waiting for transfers between devices, body(): lax.psum_scatter(grads[1], 'dp', scatter_dimension=0, tiled=True)  323 us
    reduce_scatter x1, waiting for transfers between devices, body(): lax.psum_scatter(grads[0], 'dp', scatter_dimension=0, tiled=True)  317 us
    all_gather x1, waiting for transfers between devices, body(): lax.all_gather(to_low(enc_cols), 'dp', axis=0, tiled=True)  141 us
    psum x1, waiting for transfers between devices, body(): lax.psum(shards[0].astype(jnp.bfloat16), 'grp').astype(jnp.float32)  81.2 us
    dot_general x11, matrix products, project(): jnp.einsum('...n,nm->...m', inputs, matrix, preferred_element_type=jnp.fl...  68.6 us
    dot_general x10, matrix products, project_back(): jnp.einsum('...m,nm->...n', grads, matrix, preferred_element_type=jnp.flo...  68.4 us
    scatter-add x1, other arithmetic, body(): dec_input = dec_input.at[item_rows, keep_rows].add(latent)  64.7 us
    dot_general x11, matrix products, weight_grad(): lax.dot_general(flat_in, flat_grad, (((0,), (0,)), ((), ())), preferred_e...  62.3 us
  transfers between devices with their start and end apart: 9, of which 6 were waited for; matrix products, arithmetic and copies ran while one was open for 24% of the time, Pallas kernels for 0%

commit v1 on v0

--- a/solution.py
+++ b/solution.py
@@ -20,6 +20,25 @@
 adam_eps = 1e-08
 beta_first = 0.5
 beta_second = 0.5
+
+
+def gather_around(shard, axis, dim):
+    size, mine, span = (lax.axis_size(axis), lax.axis_index(axis), shard.shape[dim])
+    right = [(i, (i + 1) % size) for i in range(size)]
+    left = [(i, (i - 1) % size) for i in range(size)]
+    out = jnp.zeros((*shard.shape[:dim], size * span, *shard.shape[dim + 1 :]), shard.dtype)
+    out = lax.dynamic_update_slice_in_dim(out, shard, mine * span, axis=dim)
+    from_left = from_right = shard
+    middle = size // 2
+    for hop in range(1, middle + 1):
+        from_left = lax.ppermute(from_left, axis, right)
+        out = lax.dynamic_update_slice_in_dim(out, from_left, (mine - hop) % size * span, axis=dim)
+        if hop < size - middle:
+            from_right = lax.ppermute(from_right, axis, left)
+            out = lax.dynamic_update_slice_in_dim(
+                out, from_right, (mine + hop) % size * span, axis=dim
+            )
+    return out
 
 
 def to_low(value):
@@ -221,7 +240,7 @@
     total_count = lax.psum(jnp.sum(group_items.astype(jnp.float32)), "grp")
     masked = total_count * (L - K)
     copies = (
-        lax.all_gather(to_low(enc_cols), "dp", axis=0, tiled=True),
+        gather_around(to_low(enc_cols), "dp", 0),
         lax.all_gather(to_low(enc_rows), "dp", axis=0, tiled=True),
         lax.all_gather(to_low(dec_cols), "dp", axis=0, tiled=True),
         lax.all_gather(to_low(dec_rows), "dp", axis=0, tiled=True),

time: 1730 us -> 1830 us (1.058)
  waiting for transfers between devices: 892 us -> 962 us
  local copies, waits for them, and re-layouts: 157 us -> 177 us
    ppermute x0 -> x7, waiting for transfers between devices: none -> 241 us  [the longest x4 169 us: gather_around(): from_left = lax.ppermute(from_left, axis, right)]
    all_gather x1 -> x0, waiting for transfers between devices: 141 us -> none  [body(): lax.all_gather(to_low(enc_cols), 'dp', axis=0, tiled=True)]
    all_gather x1, waiting for transfers between devices: 28.3 us -> 0.01 us  [body(): lax.all_gather(to_low(enc_rows), 'dp', axis=0, tiled=True)]
    convert_element_type x8 -> x7, other arithmetic: 48.9 us -> 43.7 us  [to_low(): return value.astype(jnp.bfloat16)]
  transfers between devices with their start and end apart: 9 -> 15, of which waited for: 6 -> 8; matrix products, arithmetic and copies ran while one was open for 24% -> 24% of each run, Pallas kernels for 0% -> 0%
where the time goes in v1:
time: 1830 us; the launch traced here: 1820 us
  waiting for transfers between devices  962 us (53%)
  matrix products  312 us (17%)
  other arithmetic  265 us (14%)
  local copies, waits for them, and re-layouts  177 us (10%)
  blocking collectives  67.7 us (4%)
  between operations  26 us (1%)
    reduce_scatter x1, waiting for transfers between devices, body(): lax.psum_scatter(grads[1], 'dp', scatter_dimension=0, tiled=True)  323 us
    reduce_scatter x1, waiting for transfers between devices, body(): lax.psum_scatter(grads[0], 'dp', scatter_dimension=0, tiled=True)  316 us
    ppermute x4, waiting for transfers between devices, gather_around(): from_left = lax.ppermute(from_left, axis, right)  169 us
    psum x1, waiting for transfers between devices, body(): lax.psum(shards[0].astype(jnp.bfloat16), 'grp').astype(jnp.float32)  81.2 us
    ppermute x3, waiting for transfers between devices, gather_around(): from_right = lax.ppermute(from_right, axis, left)  72.1 us
    dot_general x11, matrix products, project(): jnp.einsum('...n,nm->...m', inputs, matrix, preferred_element_type=jnp.fl...  70.2 us
    dot_general x10, matrix products, project_back(): jnp.einsum('...m,nm->...n', grads, matrix, preferred_element_type=jnp.flo...  68.6 us
    scatter-add x1, other arithmetic, body(): dec_input = dec_input.at[item_rows, keep_rows].add(latent)  65.5 us
  transfers between devices with their start and end apart: 15, of which 8 were waited for; matrix products, arithmetic and copies ran while one was open for 24% of the time, Pallas kernels for 0%

profile of v1, /device:TPU:0, one launch (start us, length us, event | category | flops | bytes accessed | tf_op | source)
XLA Modules:
  0.0 1820.8 jit_solution(11735986431292530399)
XLA Ops:
  32.8 10.9 gather_fusion.2
  46.1 10.9 gather_fusion
  57.0 10.3 broadcast_select_fusion
  71.7 46.5 %collective-permute-done = bf16[128,8192]{1,0:T(8,128)(2,1)} collective-permute-done((bf16[128,8192]{1,0:T(8,128)(2,1)}, bf16[128,8192]{1,0:T(8,128)(2,1)}, u32[]{:S(2)}, u32[]{:S(2)}) %collective-permute-start) | collective-permute-done | bytes 2097184 | tf_op jit(solution)/shard_map/ppermute | solution.py:34
  118.8 11.9 psum.63
  146.9 10.4 gather_fusion.3
  158.0 24.0 %scatter_fusion = f32[8,256]{1,0:T(8,128)S(1)} fusion(f32[8,256]{1,0:T(8,128)S(1)} %broadcast_in_dim.55, s32[512]{0:T(512)S(1)} %reshape.496, f32[512]{0:T(512)S(1)} %broadcast.514), kind=kCustom, calls=%fused_computation.5 | custom fusion | bytes 10240 | tf_op jit(solution)/shard_map/scatter | solution.py:271
  201.0 59.8 %collective-permute-done.3 = bf16[128,8192]{1,0:T(8,128)(2,1)S(1)} collective-permute-done((bf16[128,8192]{1,0:T(8,128)(2,1)}, bf16[128,8192]{1,0:T(8,128)(2,1)S(1)}, u32[]{:S(2)}, u32[]{:S(2)}) %collective-permute-start.3) | collective-permute-done | bytes 2097184 | tf_op jit(solution)/shard_map/ppermute | solution.py:37
  265.9 59.1 %collective-permute-done.4 = bf16[128,8192]{1,0:T(8,128)(2,1)S(1)} collective-permute-done((bf16[128,8192]{1,0:T(8,128)(2,1)S(1)}, bf16[128,8192]{1,0:T(8,128)(2,1)S(1)}, u32[]{:S(2)}, u32[]{:S(2)}) %collective-permute-start.4) | collective-permute-done | bytes 2097184 | tf_op jit(solution)/shard_map/ppermute | solution.py:34
  328.3 12.3 collective-permute-done.5
  342.1 63.6 %collective-permute-done.6 = bf16[128,8192]{1,0:T(8,128)(2,1)S(1)} collective-permute-done((bf16[128,8192]{1,0:T(8,128)(2,1)S(1)}, bf16[128,8192]{1,0:T(8,128)(2,1)S(1)}, u32[]{:S(2)}, u32[]{:S(2)}) %collective-permute-start.6) | collective-permute-done | bytes 2097184 | tf_op jit(solution)/shard_map/ppermute | solution.py:34
  407.2 9.7 fusion.120
  447.5 10.8 multiply_convert_fusion.2
  467.2 65.5 %scatter_fusion.1 = f32[8,256,512]{2,1,0:T(8,128)} fusion(f32[8,256,512]{2,1,0:T(8,128)} %slice_add_fusion, s32[512]{0:T(512)S(1)} %reshape.496, f32[512,512]{1,0:T(8,128)} %bitcast.272), kind=kCustom, calls=%fused_computation.6 | custom fusion | flops 262144 | bytes 3149824 | tf_op jit(solution)/shard_map/scatter-add | solution.py:273
  557.5 14.6 multiply_reduce_fusion.1
  572.1 13.8 exponential_reduce_fusion
  586.0 15.5 fusion.42
  645.6 14.0 fusion.6
  684.1 15.9 fusion.45
  700.0 23.3 %multiply_reduce_fusion = (f32[8,16,256]{2,1,0:T(8,128)S(1)}, f32[8,16,256,256]{2,3,1,0:T(8,128)}) fusion(f32[8,16,256,256]{2,3,1,0:T(8,128)} %get-tuple-element.109, f32[8,16,256]{2,1,0:T(8,128)S(1)} %log_add_fusion, bf16[8,256,16,32]{1,3,2,0:T(8,128)(2,1)} %bitcast.251, bf16[8,256,16,32]{1,3,2,0:T(8,128)(2,1)S(1)} %bitcast.249), kind=kOutput, calls=%fused_computation.10 | convolution fusion | flops 570392576 | bytes 71565312 | tf_op jit(solution)/shard_map/bqhe,bkhe->bhqk/dot_general | solution.py:169
  723.3 28.0 %multiply_convert_fusion = bf16[8,16,256,256]{2,3,1,0:T(8,128)(2,1)} fusion(f32[8,16,256,256]{2,3,1,0:T(8,128)} %get-tuple-element.121, f32[8,16,256,256]{2,3,1,0:T(8,128)} %get-tuple-element.109, f32[8,16,256]{2,1,0:T(8,128)S(1)} %get-tuple-element.120, f32[8,16,256]{2,1,0:T(8,128)S(1)} %log_add_fusion), kind=kLoop, calls=%fused_computation.9 | loop fusion | flops 41943040 | bytes 84148224 | tf_op jit(solution)/shard_map/convert_element_type | solution.py:45
  751.4 12.0 multiply_convert_fusion.6
  763.4 10.5 multiply_convert_fusion.7
  834.2 11.0 fusion.16
  845.3 9.7 multiply_reduce_fusion.19
  912.3 22.9 %pad_maximum_fusion = f32[1024,8192]{1,0:T(8,128)} fusion(f32[1024,4096]{1,0:T(8,128)} %convolution_bitcast_fusion.1, f32[1024,1024]{1,0:T(8,128)} %convolution_bitcast_fusion.6, f32[1024,3072]{1,0:T(8,128)} %convolution_bitcast_fusion.2), kind=kLoop, calls=%fused_computation.7 | loop fusion | flops 16777216 | bytes 67108864 | tf_op jit(solution)/shard_map/concatenate | solution.py:200
  961.3 18.8 %pad_maximum_fusion.1 = f32[8192,1024]{1,0:T(8,128)} fusion(f32[4096,1024]{1,0:T(8,128)S(1)} %fusion.125, f32[4096,1024]{1,0:T(8,128)} %convolution_bitcast_fusion), kind=kLoop, calls=%fused_computation.8 | loop fusion | flops 8388608 | bytes 67108864 | tf_op jit(solution)/shard_map/concatenate | solution.py:306
  984.6 316.3 %reduce-scatter.5.cloned.1.call-done = f32[128,8192]{1,0:T(8,128)} async-done(((f32[1024,8192]{1,0:T(8,128)}), f32[128,8192]{1,0:T(8,128)}) %reduce-scatter.5.cloned.1.call-update) | async-done | bytes 4194320 | tf_op jit(solution)/shard_map/reduce_scatter | solution.py:313
  1304.7 322.6 %reduce-scatter.7.cloned.1.call-done = f32[1024,1024]{1,0:T(8,128)} async-done(((f32[8192,1024]{1,0:T(8,128)}), f32[1024,1024]{1,0:T(8,128)}) %reduce-scatter.7.cloned.1.call-update) | async-done | bytes 4194320 | tf_op jit(solution)/shard_map/reduce_scatter | solution.py:314
  1632.3 38.8 %all-reduce = (f32[6,1024]{1,0:T(8,128)S(1)}, f32[7,512]{1,0:T(8,128)S(1)}, f32[]{:T(128)}) all-reduce(f32[6,1024]{1,0:T(8,128)S(1)} %concatenate.37, f32[7,512]{1,0:T(8,128)S(1)} %concatenate.38, f32[]{:T(128)} %get-tuple-element.69), channel_id=1, replica_groups=mesh['grp'=4,'dp'=8] {'grp','dp'}, use_global_device_ids=true, to_apply=%region_54.55 | all-reduce | flops 9729 | bytes 77832 | tf_op jit(solution)/shard_map/psum | solution.py:324
  1672.3 81.2 %all-reduce.4.cloned.1.call-done = (bf16[128,8192]{1,0:T(8,128)(2,1)}, bf16[1024,1024]{1,0:T(8,128)(2,1)}, bf16[64,4096]{1,0:T(8,128)(2,1)}, bf16[512,512]{1,0:T(8,128)(2,1)}) async-done(((bf16[128,8192]{1,0:T(8,128)(2,1)}, bf16[1024,1024]{1,0:T(8,128)(2,1)}, bf16[64,4096]{1,0:T(8,128)(2,1)}, bf16[512,512]{1,0:T(8,128)(2,1)}), (bf16[128,8192]{1,0:T(8,128)(2,1)}, bf16[1024,1024]{1,0:T(8,128)(2,1)}, ...) | async-done | bytes 5242896 | tf_op jit(solution)/shard_map/psum | solution.py:319
  1765.7 17.0 psum.68
  (472 shorter events, 402.8 us)
Async XLA Ops:
  7.2 400.0 %all-gather.4.cloned.1.call-start = ((), (), s32[]{:S(2)}) async-start(), calls=%async_computation.4 | async-start | bytes 18874368 | tf_op jit(solution)/shard_map/all_gather | solution.py:244
  11.3 452.6 %all-gather.6.cloned.1.call-start = ((), (), s32[]{:S(2)}) async-start(), calls=%async_computation.5 | async-start | bytes 4718592 | tf_op jit(solution)/shard_map/all_gather | solution.py:246
  13.4 524.7 %all-gather.8.cloned.1.call-start = ((), (), s32[]{:S(2)}) async-start(), calls=%async_computation.6 | async-start | bytes 4718592 | tf_op jit(solution)/shard_map/all_gather | solution.py:245
  23.1 95.2 %collective-permute-start = (bf16[128,8192]{1,0:T(8,128)(2,1)}, bf16[128,8192]{1,0:T(8,128)(2,1)}, u32[]{:S(2)}, u32[]{:S(2)}) collective-permute-start(bf16[128,8192]{1,0:T(8,128)(2,1)} %get-tuple-element.76), channel_id=1, source_target_pairs={{0,1},{1,2},{2,3},{3,4},{4,5},{5,6},{6,7},{7,0},{8,9},{9,10},{10,1... | collective-permute-start | bytes 6291464 | tf_op jit(solution)/shard_map/ppermute | solution.py:34
  23.6 168.3 %collective-permute-start.1 = (bf16[128,8192]{1,0:T(8,128)(2,1)}, bf16[128,8192]{1,0:T(8,128)(2,1)}, u32[]{:S(2)}, u32[]{:S(2)}) collective-permute-start(bf16[128,8192]{1,0:T(8,128)(2,1)} %get-tuple-element.76), channel_id=1, source_target_pairs={{0,7},{1,0},{2,1},{3,2},{4,3},{5,4},{6,5},{7,6},{8,15},{9,8},{10,9... | collective-permute-start | bytes 6291464 | tf_op jit(solution)/shard_map/ppermute | solution.py:37
  28.8 951.4 %reduce-scatter.9.cloned.1.call-start = ((), (), s32[]{:S(2)}) async-start(), calls=%async_computation.9 | async-start | bytes 9437184 | tf_op jit(solution)/shard_map/reduce_scatter | solution.py:315
  29.0 117.8 %copy-start.6 = (s32[512]{0:T(512)}, s32[512]{0:T(512)S(1)}, u32[]{:S(2)}) copy-start(s32[512]{0:T(512)S(1)} %reshape.472) | copy-start | bytes 6148
  32.7 374.5 %copy-start.109 = (pred[8,64]{1,0:T(8,128)(4,1)}, pred[8,64]{1,0:T(8,128)(4,1)S(1)}, u32[]{:S(2)}) copy-start(pred[8,64]{1,0:T(8,128)(4,1)S(1)} %get-tuple-element.74) | copy-start | bytes 1540
  118.2 76.5 %collective-permute-start.2 = (bf16[128,8192]{1,0:T(8,128)(2,1)}, bf16[128,8192]{1,0:T(8,128)(2,1)S(1)}, u32[]{:S(2)}, u32[]{:S(2)}) collective-permute-start(bf16[128,8192]{1,0:T(8,128)(2,1)} %collective-permute-done), channel_id=1, source_target_pairs={{0,1},{1,2},{2,3},{3,4},{4,5},{5,6},{6,7},{7,0},{8,9},{9,10},{10,1... | collective-permute-start | bytes 6291464 | tf_op jit(solution)/shard_map/ppermute | solution.py:34
  185.7 352.4 %copy-start.106 = (f32[1,512]{1,0:T(1,128)}, f32[1,512]{1,0:T(1,128)S(1)}, u32[]{:S(2)}) copy-start(f32[1,512]{1,0:T(1,128)S(1)} %get-tuple-element.93) | copy-start | bytes 6148
  185.7 352.4 %copy-start.121 = (f32[1,512]{1,0:T(1,128)}, f32[1,512]{1,0:T(1,128)S(1)}, u32[]{:S(2)}) copy-start(f32[1,512]{1,0:T(1,128)S(1)} %get-tuple-element.92) | copy-start | bytes 6148
  185.8 231.6 %copy-start.64 = (f32[1,1024]{1,0:T(1,128)}, f32[1,1024]{1,0:T(1,128)S(1)}, u32[]{:S(2)}) copy-start(f32[1,1024]{1,0:T(1,128)S(1)} %get-tuple-element.87) | copy-start | bytes 12292
  185.8 231.6 %copy-start.68 = (f32[1,1024]{1,0:T(1,128)}, f32[1,1024]{1,0:T(1,128)S(1)}, u32[]{:S(2)}) copy-start(f32[1,1024]{1,0:T(1,128)S(1)} %get-tuple-element.86) | copy-start | bytes 12292
  185.8 261.6 %copy-start.93 = (f32[1,1024]{1,0:T(1,128)}, f32[1,1024]{1,0:T(1,128)S(1)}, u32[]{:S(2)}) copy-start(f32[1,1024]{1,0:T(1,128)S(1)} %get-tuple-element.85) | copy-start | bytes 12292
  185.8 261.6 %copy-start.115 = (f32[1,1024]{1,0:T(1,128)}, f32[1,1024]{1,0:T(1,128)S(1)}, u32[]{:S(2)}) copy-start(f32[1,1024]{1,0:T(1,128)S(1)} %get-tuple-element.84) | copy-start | bytes 12292
  185.8 278.1 %copy-start.100 = (f32[1,1024]{1,0:T(1,128)}, f32[1,1024]{1,0:T(1,128)S(1)}, u32[]{:S(2)}) copy-start(f32[1,1024]{1,0:T(1,128)S(1)} %get-tuple-element.83) | copy-start | bytes 12292
  185.8 278.1 %copy-start.117 = (f32[1,1024]{1,0:T(1,128)}, f32[1,1024]{1,0:T(1,128)S(1)}, u32[]{:S(2)}) copy-start(f32[1,1024]{1,0:T(1,128)S(1)} %get-tuple-element.88) | copy-start | bytes 12292
  191.9 68.9 %collective-permute-start.3 = (bf16[128,8192]{1,0:T(8,128)(2,1)}, bf16[128,8192]{1,0:T(8,128)(2,1)S(1)}, u32[]{:S(2)}, u32[]{:S(2)}) collective-permute-start(bf16[128,8192]{1,0:T(8,128)(2,1)} %collective-permute-done.1), channel_id=1, source_target_pairs={{0,7},{1,0},{2,1},{3,2},{4,3},{5,4},{6,5},{7,6},{8,15},{9,8},{10,9... | collective-permute-start | bytes 6291464 | tf_op jit(solution)/shard_map/ppermute | solution.py:37
  194.8 130.2 %collective-permute-start.4 = (bf16[128,8192]{1,0:T(8,128)(2,1)S(1)}, bf16[128,8192]{1,0:T(8,128)(2,1)S(1)}, u32[]{:S(2)}, u32[]{:S(2)}) collective-permute-start(bf16[128,8192]{1,0:T(8,128)(2,1)S(1)} %collective-permute-done.2), channel_id=1, source_target_pairs={{0,1},{1,2},{2,3},{3,4},{4,5},{5,6},{6,7},{7,0},{8,9},{9,10},{10,1... | collective-permute-start | bytes 6291464 | tf_op jit(solution)/shard_map/ppermute | solution.py:34
  260.8 79.8 %collective-permute-start.5 = (bf16[128,8192]{1,0:T(8,128)(2,1)S(1)}, bf16[128,8192]{1,0:T(8,128)(2,1)S(1)}, u32[]{:S(2)}, u32[]{:S(2)}) collective-permute-start(bf16[128,8192]{1,0:T(8,128)(2,1)S(1)} %collective-permute-done.3), channel_id=1, source_target_pairs={{0,7},{1,0},{2,1},{3,2},{4,3},{5,4},{6,5},{7,6},{8,15},{9,8},{10,9... | collective-permute-start | bytes 6291464 | tf_op jit(solution)/shard_map/ppermute | solution.py:37
  325.0 80.7 %collective-permute-start.6 = (bf16[128,8192]{1,0:T(8,128)(2,1)S(1)}, bf16[128,8192]{1,0:T(8,128)(2,1)S(1)}, u32[]{:S(2)}, u32[]{:S(2)}) collective-permute-start(bf16[128,8192]{1,0:T(8,128)(2,1)S(1)} %collective-permute-done.4), channel_id=1, source_target_pairs={{0,1},{1,2},{2,3},{3,4},{4,5},{5,6},{6,7},{7,0},{8,9},{9,10},{10,1... | collective-permute-start | bytes 6291464 | tf_op jit(solution)/shard_map/ppermute | solution.py:34
  795.9 186.6 %reduce-scatter.11.cloned.1.call-start = ((), (), s32[]{:S(2)}) async-start(), calls=%async_computation.10 | async-start | bytes 9437184 | tf_op jit(solution)/shard_map/reduce_scatter | solution.py:316
  828.9 472.0 %reduce-scatter.5.cloned.1.call-start = ((), (), s32[]{:S(2)}) async-start(), calls=%async_computation.7 | async-start | bytes 37748736 | tf_op jit(solution)/shard_map/reduce_scatter | solution.py:313
  935.2 692.1 %reduce-scatter.7.cloned.1.call-start = ((), (), s32[]{:S(2)}) async-start(), calls=%async_computation.8 | async-start | bytes 37748736 | tf_op jit(solution)/shard_map/reduce_scatter | solution.py:314
  980.1 773.4 %all-reduce.4.cloned.1.call-start = ((), (), s32[]{:S(2)}) async-start(), calls=%async_computation.11 | async-start | bytes 10485760 | tf_op jit(solution)/shard_map/psum | solution.py:319
  1631.2 153.5 %copy-start.80 = (f32[7,512]{1,0:T(8,128)S(1)}, f32[7,512]{1,0:T(8,128)}, u32[]{:S(2)}) copy-start(f32[7,512]{1,0:T(8,128)} %param.37) | copy-start | bytes 43012
  1631.2 153.5 %copy-start.97 = (f32[7,512]{1,0:T(8,128)S(1)}, f32[7,512]{1,0:T(8,128)}, u32[]{:S(2)}) copy-start(f32[7,512]{1,0:T(8,128)} %param.43) | copy-start | bytes 43012
  1631.3 153.5 %copy-start.98 = (f32[7,512]{1,0:T(8,128)S(1)}, f32[7,512]{1,0:T(8,128)}, u32[]{:S(2)}) copy-start(f32[7,512]{1,0:T(8,128)} %param.49) | copy-start | bytes 43012
  1631.3 154.2 %copy-start.72 = (f32[6,1024]{1,0:T(8,128)S(1)}, f32[6,1024]{1,0:T(8,128)}, u32[]{:S(2)}) copy-start(f32[6,1024]{1,0:T(8,128)} %param.36) | copy-start | bytes 73732
  1631.3 154.2 %copy-start.88 = (f32[6,1024]{1,0:T(8,128)S(1)}, f32[6,1024]{1,0:T(8,128)}, u32[]{:S(2)}) copy-start(f32[6,1024]{1,0:T(8,128)} %param.42) | copy-start | bytes 73732
  1631.3 154.1 %copy-start.89 = (f32[6,1024]{1,0:T(8,128)S(1)}, f32[6,1024]{1,0:T(8,128)}, u32[]{:S(2)}) copy-start(f32[6,1024]{1,0:T(8,128)} %param.48) | copy-start | bytes 73732
  1631.3 154.8 %copy-start.50 = (f32[512,512]{1,0:T(8,128)S(1)}, f32[512,512]{1,0:T(8,128)}, u32[]{:S(2)}) copy-start(f32[512,512]{1,0:T(8,128)} %param.35) | copy-start | bytes 3145732
  (126 other events, 1092.7 us)
Sparse Core Ops, SparseCore 0:
  11.4 235.4 all-gather.3
  249.1 77.5 all-gather.5
  328.8 67.1 all-gather.7
  796.0 88.5 reduce-scatter.8
  886.8 87.9 reduce-scatter.10
  977.0 323.8 reduce-scatter.4
  1303.4 323.8 reduce-scatter.6
  1632.2 121.2 all-reduce.3
